TPU v7x, 32 devices: a whole 2x2x4 slice. The times are simulated.
32 devices in a mesh: shard: 4 (over z), tensor: 4 (over x, core), dp: 2 (over y).
Axes of the slice: x: 2, y: 2, z: 4, core: 2. Of those that a mesh axis runs over, the one named last changes fastest.
Arguments:
- gradient: bfloat16 [1, 8192, 8192], P(None, 'shard', ('tensor', 'dp')), may hold values from -16 to 16
- momentum: float32 [1, 8192, 8192], P(None, 'shard', ('tensor', 'dp')), may hold values from -16 to 16
- prior_right_factor: float32 [1, 8192, 128], P(None, ('tensor', 'dp')), may hold values from -8 to 8
Outputs:
- momentum_next: float32 [1, 8192, 8192], P(None, 'shard', ('tensor', 'dp'))
- following_right_factor: float32 [1, 8192, 128], P(None, ('tensor', 'dp'))
- direction: bfloat16 [1, 8192, 8192], P(None, 'shard', ('tensor', 'dp'))
All inputs are finite; a program needn't handle non-finite values.
Results may differ from a plain program's by a relative error of at most 0.0029.
Values sent between devices are 32-bit elements; how exact they have to be, the bound alone decides.
A program may use at most 64 MiB of HBM per device.

v0:
```python
import jax
import jax.numpy as jnp
from jax import lax
from jax.sharding import PartitionSpec as P

M = 8192
N = 8192
R = 128


decay_rate = 0.95
epsilon = 1e-06


def cholesky_pass(row_segment_block, summer):
    gram_matrix = summer(
        jnp.einsum(
            "ktp,ktv->kpv", row_segment_block, row_segment_block, precision=lax.Precision.HIGHEST
        )
    )
    factor_lower = jnp.linalg.cholesky(gram_matrix)
    return lax.linalg.triangular_solve(
        factor_lower, row_segment_block, left_side=False, lower=True, transpose_a=True
    )


def shards(gradient, momentum, prior_right_factor):
    mixed_update = momentum + gradient.astype(jnp.float32)
    partial_value = jnp.einsum(
        "aph,aht->apt", mixed_update, prior_right_factor, precision=lax.Precision.HIGHEST
    )
    left_full = lax.psum(partial_value, ("tensor", "dp"))

    def summer(operand):
        return lax.psum(operand, "shard")

    column_basis = cholesky_pass(cholesky_pass(left_full, summer), summer)
    right_portion = jnp.einsum(
        "wvp,wvc->wpc", mixed_update, column_basis, precision=lax.Precision.HIGHEST
    )
    fresh_right_factor = lax.psum(right_portion, "shard")
    momentum_next = mixed_update - (1.0 - decay_rate) * jnp.einsum(
        "fwd,fad->fwa", column_basis, fresh_right_factor, precision=lax.Precision.HIGHEST
    )
    squares = lax.psum(jnp.sum(fresh_right_factor * fresh_right_factor, axis=1), ("tensor", "dp"))
    scales = jnp.sqrt(squares / N + epsilon)
    following_right_factor = fresh_right_factor / scales[:, None, :]
    direction = jnp.sqrt(M / R) * jnp.einsum(
        "fwd,fad->fwa", column_basis, following_right_factor, precision=lax.Precision.HIGHEST
    )
    return (momentum_next, following_right_factor, direction.astype(jnp.bfloat16))


def solution(mesh):
    return jax.shard_map(
        shards,
        mesh=mesh,
        in_specs=(
            P(None, "shard", ("tensor", "dp")),
            P(None, "shard", ("tensor", "dp")),
            P(None, ("tensor", "dp"), None),
        ),
        out_specs=(
            P(None, "shard", ("tensor", "dp")),
            P(None, ("tensor", "dp"), None),
            P(None, "shard", ("tensor", "dp")),
        ),
        check_vma=False,
    )
```

profile of v0, /device:TPU:0, one launch (start us, length us, event | category | flops | bytes accessed | tf_op | source)
XLA Modules:
  0.0 303.4 jit_solution(12803602012103822525)
XLA Ops:
  7.2 0.0 copy-start
  7.2 0.0 all-reduce.5.cloned.1.call-start
  7.2 1.0 copy-done
  8.2 10.7 %fusion.5 = f32[1,2048,128]{2,1,0:T(8,128)} fusion(f32[1,2048,1024]{2,1,0:T(8,128)} %param.7, bf16[1,2048,1024]{2,1,0:T(8,128)(2,1)} %param.6, f32[1,1024,128]{2,1,0:T(8,128)S(1)} %copy-done), kind=kOutput, calls=%fused_computation.8 | convolution fusion | flops 3225419776 | bytes 14155776 | tf_op jit(solution)/shard_map/aph,aht->apt/dot_general | solution.py:29
  19.0 0.0 all-reduce.5.cloned.1.call-update
  19.0 0.0 all-reduce.7.cloned.1.call-start
  19.0 59.5 %all-reduce.5.cloned.1.call-done = f32[1,2048,128]{2,1,0:T(8,128)} async-done(((f32[1,2048,128]{2,1,0:T(8,128)}), f32[1,2048,128]{2,1,0:T(8,128)}) %all-reduce.5.cloned.1.call-update) | async-done | bytes 1048592 | tf_op jit(solution)/shard_map/psum | solution.py:32
  78.6 4.0 %convolution_bitcast_fusion.3 = f32[1,128,128]{1,2,0:T(8,128)} fusion(f32[1,2048,128]{2,1,0:T(8,128)} %all-reduce.5.cloned.1.call-done), kind=kOutput, calls=%fused_computation.13 | convolution fusion | flops 402653184 | bytes 1114112 | tf_op jit(solution)/shard_map/ktp,ktv->kpv/dot_general | solution.py:17
  82.5 0.0 all-reduce.7.cloned.1.call-update
  82.6 0.2 all-reduce.9.cloned.1.call-start
  82.8 33.5 %all-reduce.7.cloned.1.call-done = f32[1,128,128]{1,2,0:T(8,128)} async-done(((f32[1,128,128]{1,2,0:T(8,128)}), f32[1,128,128]{1,2,0:T(8,128)}) %all-reduce.7.cloned.1.call-update) | async-done | bytes 65552 | tf_op jit(solution)/shard_map/psum | solution.py:35
  116.3 0.9 copy.7
  117.2 0.9 fusion.21
  118.1 11.7 %custom-call.8 = f32[1,128,128]{2,1,0:T(8,128)S(1)} custom-call(f32[1,128,128]{2,1,0:T(8,128)S(1)} %fusion.21), custom_call_target="Cholesky" | custom-call | tf_op jit(solution)/shard_map/jit(cholesky)/cholesky | solution.py:21
  129.8 0.6 compare_reduce_fusion.1
  130.4 0.7 fusion.16
  131.1 9.8 %custom-call.9 = f32[1,1,128,128]{2,3,1,0:T(8,128)S(1)} custom-call(f32[1,1,128,128]{3,2,1,0:T(8,128)S(1)} %fusion.16), custom_call_target="InvertDiagBlocksLowerTriangular" | custom-call | tf_op jit(solution)/shard_map/triangular_solve/custom-call.0 | solution.py:22
  140.9 2.3 convolution_bitcast_fusion.1
  143.2 1.6 convolution_bitcast_fusion.2
  144.8 0.0 all-reduce.9.cloned.1.call-update
  144.9 0.3 all-reduce.11.cloned.1.call-start
  145.1 33.9 %all-reduce.9.cloned.1.call-done = f32[1,128,128]{1,2,0:T(8,128)} async-done(((f32[1,128,128]{1,2,0:T(8,128)}), f32[1,128,128]{1,2,0:T(8,128)}) %all-reduce.9.cloned.1.call-update) | async-done | bytes 65552 | tf_op jit(solution)/shard_map/psum | solution.py:35
  179.0 0.9 copy.9
  179.9 0.9 fusion.19
  180.8 11.7 %custom-call.10 = f32[1,128,128]{2,1,0:T(8,128)S(1)} custom-call(f32[1,128,128]{2,1,0:T(8,128)S(1)} %fusion.19), custom_call_target="Cholesky" | custom-call | tf_op jit(solution)/shard_map/jit(cholesky)/cholesky | solution.py:21
  192.5 0.6 compare_reduce_fusion
  193.2 0.7 fusion.17
  193.8 9.8 %custom-call.11 = f32[1,1,128,128]{2,3,1,0:T(8,128)S(1)} custom-call(f32[1,1,128,128]{3,2,1,0:T(8,128)S(1)} %fusion.17), custom_call_target="InvertDiagBlocksLowerTriangular" | custom-call | tf_op jit(solution)/shard_map/triangular_solve/custom-call.0 | solution.py:22
  203.7 1.1 convolution_bitcast_fusion
  204.7 17.3 %fusion.8 = f32[1,1024,128]{2,1,0:T(8,128)} fusion(f32[2048,128]{0,1:T(8,128)S(1)} %convolution_bitcast_fusion, f32[1,2048,1024]{2,1,0:T(8,128)} %param.7, bf16[1,2048,1024]{2,1,0:T(8,128)(2,1)} %param.6), kind=kOutput, calls=%fused_computation.11 | convolution fusion | flops 3225419776 | bytes 14155776 | tf_op jit(solution)/shard_map/wvp,wvc->wpc/dot_general | solution.py:38
  222.0 0.0 all-reduce.11.cloned.1.call-update
  222.0 38.4 %all-reduce.11.cloned.1.call-done = f32[1,1024,128]{2,1,0:T(8,128)} async-done(((f32[1,1024,128]{2,1,0:T(8,128)}), f32[1,1024,128]{2,1,0:T(8,128)}) %all-reduce.11.cloned.1.call-update) | async-done | bytes 524304 | tf_op jit(solution)/shard_map/psum | solution.py:41
  260.4 1.2 multiply_reduce_fusion
  261.6 13.4 %psum.39 = f32[1,128]{1,0:T(1,128)S(1)} all-reduce(f32[1,128]{1,0:T(1,128)S(1)} %bitcast.76), channel_id=1, replica_groups=mesh['shard'=4,'tensor'=4,'dp'=2] {'tensor','dp'}, use_global_device_ids=true, to_apply=%region_7.10 | all-reduce | flops 128 | bytes 1024 | tf_op jit(solution)/shard_map/psum | solution.py:45
  275.0 0.0 copy-start.1
  275.0 1.2 broadcast_divide_fusion
  276.2 0.0 copy-start.2
  276.2 8.4 %fusion.4 = bf16[1,2048,1024]{2,1,0:T(8,128)(2,1)} fusion(f32[2048,128]{0,1:T(8,128)S(1)} %convolution_bitcast_fusion, f32[1,1024,128]{2,1,0:T(8,128)S(1)} %broadcast_divide_fusion), kind=kOutput, calls=%fused_computation.7 | convolution fusion | flops 3225419776 | bytes 5767168 | tf_op jit(solution)/shard_map/fwd,fad->fwa/dot_general | solution.py:48
  284.6 0.0 copy-done.1
  284.6 12.2 %bitcast_subtract_fusion = f32[1,2048,1024]{2,1,0:T(8,128)} fusion(f32[2048,128]{0,1:T(8,128)S(1)} %convolution_bitcast_fusion, f32[1,2048,1024]{2,1,0:T(8,128)} %param.7, bf16[1,2048,1024]{2,1,0:T(8,128)(2,1)S(1)} %copy-done.1, f32[1,1024,128]{2,1,0:T(8,128)} %all-reduce.11.cloned.1.call-done), kind=kOutput, calls=%fused_computation | convolution fusion | flops 3229614080 | bytes 22544384 | tf_op jit(solution)/shard_map/fwd,fad->fwa/dot_general | solution.py:42
  296.8 0.0 copy-done.2
  (3 shorter events, 0.1 us)
Async XLA Ops:
  7.2 1.0 copy-start
  7.2 71.4 %all-reduce.5.cloned.1.call-start = ((), (), s32[]{:S(2)}) async-start(), calls=%async_computation | async-start | bytes 2097152 | tf_op jit(solution)/shard_map/psum | solution.py:32
  19.0 97.3 %all-reduce.7.cloned.1.call-start = ((), (), s32[]{:S(2)}) async-start(), calls=%async_computation.1 | async-start | bytes 131072 | tf_op jit(solution)/shard_map/psum | solution.py:35
  82.6 96.4 %all-reduce.9.cloned.1.call-start = ((), (), s32[]{:S(2)}) async-start(), calls=%async_computation.2 | async-start | bytes 131072 | tf_op jit(solution)/shard_map/psum | solution.py:35
  144.9 115.5 %all-reduce.11.cloned.1.call-start = ((), (), s32[]{:S(2)}) async-start(), calls=%async_computation.3 | async-start | bytes 1048576 | tf_op jit(solution)/shard_map/psum | solution.py:41
  275.0 9.7 %copy-start.1 = (bf16[1,2048,1024]{2,1,0:T(8,128)(2,1)S(1)}, bf16[1,2048,1024]{2,1,0:T(8,128)(2,1)}, u32[]{:S(2)}) copy-start(bf16[1,2048,1024]{2,1,0:T(8,128)(2,1)} %param.6) | copy-start | bytes 12582916
  276.2 20.6 %copy-start.2 = (f32[1,1024,128]{2,1,0:T(8,128)}, f32[1,1024,128]{2,1,0:T(8,128)S(1)}, u32[]{:S(2)}) copy-start(f32[1,1024,128]{2,1,0:T(8,128)S(1)} %broadcast_divide_fusion) | copy-start | bytes 1572868
Sparse Core Ops, SparseCore 0:
  19.1 59.4 all-reduce.4
  82.7 33.5 all-reduce.6
  145.0 33.9 all-reduce.8
  222.1 38.1 all-reduce.10
where the time goes:
time: 304 us; the launch traced here: 303 us
  waiting for transfers between devices  165 us (54%)
  matrix products  57.6 us (19%)
  other arithmetic  49.9 us (16%)
  between operations  13.9 us (5%)
  blocking collectives  13.4 us (4%)
    psum x2, waiting for transfers between devices, summer(): return lax.psum(operand, 'shard')  67.3 us
    psum x1, waiting for transfers between devices, shards(): left_full = lax.psum(partial_value, ('tensor', 'dp'))  59.5 us
    psum x1, waiting for transfers between devices, shards(): fresh_right_factor = lax.psum(right_portion, 'shard')  38.4 us
    another operation x6, other arithmetic, cholesky_pass(): factor_lower = jnp.linalg.cholesky(gram_matrix)  24.8 us
    another operation x4, other arithmetic, cholesky_pass(): lax.linalg.triangular_solve(factor_lower, row_segment_block, left_side=Fa...  20.9 us
    dot_general x1, matrix products, shards(): jnp.einsum('wvp,wvc->wpc', mixed_update, column_basis, precision=lax.Prec...  17.3 us
    psum x1, blocking collectives, shards(): lax.psum(jnp.sum(fresh_right_factor * fresh_right_factor, axis=1), ('tens...  13.4 us
    dot_general x1, matrix products, shards(): jnp.einsum('fwd,fad->fwa', column_basis, fresh_right_factor, precision=la...  12.2 us
  transfers between devices with their start and end apart: 4, of which 4 were waited for; matrix products, arithmetic and copies ran while one was open for 0% of the time, Pallas kernels for 0%

commit v1 on v0

v1 whole, which is shorter than its diff:
```python
import functools

import jax
import jax.numpy as jnp
from jax import lax
from jax.experimental import pallas as pl
from jax.experimental.pallas import tpu as pltpu
from jax.sharding import PartitionSpec as P

MESH = pl.DeviceIdType.MESH
HIGHEST = lax.Precision.HIGHEST
decay_rate = 0.95
epsilon = 1e-06
CHUNKS = 8


def dot(a, b, dims, precision=HIGHEST):
    return lax.dot_general(
        a, b, (dims, ((), ())), precision=precision, preferred_element_type=jnp.float32
    )


def split(value):
    high = value.astype(jnp.bfloat16)
    low = (value - high.astype(jnp.float32)).astype(jnp.bfloat16)
    return high, low


def inverse_factor(gram):
    size = gram.shape[0]
    sub = lax.broadcasted_iota(jnp.int32, (8, size), 0)
    lane = lax.broadcasted_iota(jnp.int32, (8, size), 1)
    rows = lax.broadcasted_iota(jnp.int32, (size, size), 0)
    lanes = lax.broadcasted_iota(jnp.int32, (size, size), 1)

    def row(value, index):
        return jnp.broadcast_to(value[index : index + 1], value.shape)

    def block(step, a):
        top = a[:8]
        columns = [jnp.broadcast_to(top[:, c : c + 1], (8, size)) for c in range(8)]
        panel = jnp.where(lane < 8, jnp.where(lane == sub, 1.0, 0.0), top)
        scale = jnp.zeros((8, size), jnp.float32)
        for c in range(8):
            inverse_root = lax.rsqrt(row(columns[c], c))
            scale = jnp.where(sub == c, inverse_root, scale)
            factor = jnp.where(sub > c, columns[c] * (inverse_root * inverse_root), 0.0)
            panel = panel - factor * row(panel, c)
            for j in range(c + 1, 8):
                columns[j] = columns[j] - factor * row(columns[j], c)
        square = scale * scale
        solved = panel * square
        for c in range(7, 0, -1):
            solved = solved - jnp.where(sub < c, columns[c] * square, 0.0) * row(solved, c)
        active = rows < size - 8 * step
        source = jnp.where(active, a, 0.0)[8:]
        rest = jnp.where(active & (lanes < 8), 0.0, a)[8:]
        for c in range(8):
            rest = rest - jnp.broadcast_to(source[:, c : c + 1], rest.shape) * jnp.broadcast_to(
                solved[c : c + 1], rest.shape
            )
        return pltpu.roll(jnp.concatenate([rest, panel * scale], axis=0), size - 8, 1)

    return jnp.where(rows >= lanes, lax.fori_loop(0, size // 8, block, gram), 0.0)


class Group:
    def __init__(self, count, me, where):
        self.count, self.me, self.where = count, me, where

    def peer(self, k):
        other = lax.rem(self.me + k, self.count)
        return other, self.where(other)


def groups(shape):
    s, t, d = lax.axis_index("shard"), lax.axis_index("tensor"), lax.axis_index("dp")
    tensor, dp = shape["tensor"], shape["dp"]
    cores = 2 if tensor % 2 == 0 else 1
    core, x = lax.rem(t, cores), lax.div(t, cores)
    return {
        "core": Group(cores, core, lambda j: {"tensor": x * cores + j}),
        "x": Group(tensor // cores, x, lambda j: {"tensor": j * cores + core}),
        "y": Group(dp, d, lambda j: {"dp": j}),
        "z": Group(shape["shard"], s, lambda j: {"shard": j}),
        "plane": Group(
            tensor * dp, t * dp + d, lambda j: {"tensor": lax.div(j, dp), "dp": lax.rem(j, dp)}
        ),
    }


def stage_plan(shape, rows):
    cores = 2 if shape["tensor"] % 2 == 0 else 1
    sizes = {"core": cores, "x": shape["tensor"] // cores, "y": shape["dp"]}
    members = shape["tensor"] * shape["dp"]
    halves = 2 if rows % (16 * members) == 0 else 1
    orders = (("core", "x", "y"), ("core", "y", "x"))[:halves]
    return sizes, halves, orders


def factors(shape, momentum_ref, gradient_ref, prior_ref, basis_ref, right_ref, following_ref, *scratch):
    (mixed, raw, left, whole, local, grams, shares, share_in, squares, load_sem, gram_send, gram_recv, share_send,
     share_recv, full_send, full_recv, square_send, square_recv, *stages) = scratch
    rows, cols = mixed.shape
    rank = prior_ref.shape[1]
    where = groups(shape)
    sizes, halves, orders = stage_plan(shape, rows)
    part = rows // CHUNKS

    def load(i):
        at = pl.ds(pl.multiple_of(i * part, 8), part)
        return (
            pltpu.make_async_copy(momentum_ref.at[at], mixed.at[at], load_sem.at[0, i]),
            pltpu.make_async_copy(gradient_ref.at[at], raw.at[at], load_sem.at[1, i]),
        )

    for i in range(CHUNKS):
        for copy in load(i):
            copy.start()

    barrier = pltpu.get_barrier_semaphore()
    peers = 0
    for name in ("plane", "z"):
        for k in range(1, where[name].count):
            pl.semaphore_signal(barrier, inc=1, device_id=where[name].peer(k)[1], device_id_type=MESH)
            peers += 1
    pl.semaphore_wait(barrier, peers)

    prior = prior_ref[...]

    def first(i, carry):
        for copy in load(i):
            copy.wait()
        at = pl.ds(pl.multiple_of(i * part, 8), part)
        value = mixed[at, :] + raw[at, :].astype(jnp.float32)
        mixed[at, :] = value
        left[at, :] = dot(value, prior, ((1,), (0,)))
        return carry

    lax.fori_loop(0, CHUNKS, first, 0)

    starts = [h * (rows // halves) for h in range(halves)]
    sizes_now = [rows // halves] * halves
    trail = []
    for level in range(3):
        pending = []
        for h in range(halves):
            name = orders[h][level]
            group = where[name]
            buffer, send_sem, recv_sem = stages[level * 6 + h * 3 : level * 6 + h * 3 + 3] if halves == 2 else stages[level * 3 : level * 3 + 3]
            if group.count == 1:
                continue
            size = sizes_now[h] // group.count
            copies = []
            for k in range(1, group.count):
                other, device = group.peer(k)
                copy = pltpu.make_async_remote_copy(
                    src_ref=left.at[pl.ds(pl.multiple_of(starts[h] + other * size, 8), size)],
                    dst_ref=buffer.at[k - 1],
                    send_sem=send_sem.at[k - 1],
                    recv_sem=recv_sem.at[k - 1],
                    device_id=device,
                    device_id_type=MESH,
                )
                copy.start()
                copies.append(copy)
            pending.append((h, group, size, copies, buffer))
        for h, group, size, copies, buffer in pending:
            for copy in copies:
                copy.wait()
            own = pl.multiple_of(starts[h] + group.me * size, 8)
            total = left[pl.ds(own, size), :]
            for k in range(group.count - 1):
                total = total + buffer[k]
            left[pl.ds(own, size), :] = total
            starts[h], sizes_now[h] = own, size
            trail.append((level, h, group, own, size))
    for h in range(halves):
        own = pl.ds(starts[h], sizes_now[h])
        whole[own, :] = left[own, :]
    for level in (2, 1, 0):
        copies = []
        for stage, h, group, own, size in trail:
            if stage != level:
                continue
            index = (level * 2 + h) if halves == 2 else level
            for k in range(1, group.count):
                other, device = group.peer(k)
                at = pl.ds(own, size)
                copy = pltpu.make_async_remote_copy(
                    src_ref=whole.at[at],
                    dst_ref=whole.at[at],
                    send_sem=full_send.at[index, k - 1],
                    recv_sem=full_recv.at[index, k - 1],
                    device_id=device,
                    device_id_type=MESH,
                )
                copy.start()
                copies.append(copy)
        for copy in copies:
            copy.wait()

    def exchange(slots, group, send_sem, recv_sem):
        copies = []
        for k in range(1, group.count):
            copy = pltpu.make_async_remote_copy(
                src_ref=slots.at[group.me],
                dst_ref=slots.at[group.me],
                send_sem=send_sem.at[k - 1],
                recv_sem=recv_sem.at[k - 1],
                device_id=group.peer(k)[1],
                device_id_type=MESH,
            )
            copy.start()
            copies.append(copy)
        return copies

    def summed(slots, count):
        total = slots[0]
        for i in range(1, count):
            total = total + slots[i]
        return total

    z = where["z"]
    value = whole[...]
    grams[0, z.me] = dot(value, value, ((0,), (0,)))
    for copy in exchange(grams.at[0], z, gram_send.at[0], gram_recv.at[0]):
        copy.wait()
    inverse = inverse_factor(summed(grams.at[0], z.count))
    value = dot(whole[...], inverse, ((1,), (1,)))
    basis_ref[...] = value
    grams[1, z.me] = dot(value, value, ((0,), (0,)))
    gram_copies = exchange(grams.at[1], z, gram_send.at[1], gram_recv.at[1])

    local[...] = dot(value, mixed[...], ((0,), (0,)))
    share = rank // z.count
    share_copies = []
    for k in range(1, z.count):
        other, device = z.peer(k)
        copy = pltpu.make_async_remote_copy(
            src_ref=local.at[pl.ds(pl.multiple_of(other * share, 8), share)],
            dst_ref=share_in.at[k - 1],
            send_sem=share_send.at[k - 1],
            recv_sem=share_recv.at[k - 1],
            device_id=device,
            device_id_type=MESH,
        )
        copy.start()
        share_copies.append(copy)
    for copy in gram_copies:
        copy.wait()
    inverse = inverse_factor(summed(grams.at[1], z.count))
    for copy in share_copies:
        copy.wait()
    total = local[pl.ds(pl.multiple_of(z.me * share, 8), share), :]
    for k in range(z.count - 1):
        total = total + share_in[k]
    shares[z.me] = total
    full = exchange(shares, z, full_send.at[full_send.shape[0] - 1], full_recv.at[full_recv.shape[0] - 1])
    basis_ref[...] = dot(basis_ref[...], inverse, ((1,), (1,)))
    for copy in full:
        copy.wait()
    stacked = jnp.concatenate([shares[i] for i in range(z.count)], axis=0)
    right = dot(stacked, inverse, ((0,), (1,)))
    right_ref[...] = right
    plane = where["plane"]
    squares[plane.me] = jnp.broadcast_to(jnp.sum(right * right, axis=0, keepdims=True), (8, rank))
    for copy in exchange(squares, plane, square_send, square_recv):
        copy.wait()
    mean = summed(squares, plane.count)[:1] / (cols * plane.count)
    following_ref[...] = right / jnp.sqrt(mean + epsilon)


def finish(scale, momentum_ref, gradient_ref, basis_ref, right_ref, following_ref, next_ref, direction_ref):
    high, low = split(basis_ref[...])
    right = right_ref[...].astype(jnp.bfloat16)
    follow_high, follow_low = split(following_ref[...])
    dims = ((1,), (1,))
    next_ref[...] = (
        momentum_ref[...]
        + gradient_ref[...].astype(jnp.float32)
        - (1.0 - decay_rate) * dot(high, right, dims, None)
    )
    product = dot(high, follow_high, dims, None) + (
        dot(high, follow_low, dims, None) + dot(low, follow_high, dims, None)
    )
    direction_ref[...] = (scale * product).astype(jnp.bfloat16)


def shards(shape, gradient, momentum, prior_right_factor):
    gradient, momentum, prior = gradient[0], momentum[0], prior_right_factor[0]
    rows, cols = momentum.shape
    rank = prior.shape[1]
    sizes, halves, orders = stage_plan(shape, rows)
    stages = []
    now = [rows // halves] * halves
    widest = max(max(sizes.values()), shape["shard"], 2) - 1
    for level in range(3):
        for h in range(halves):
            count = sizes[orders[h][level]]
            now[h] //= count
            stages += [
                pltpu.VMEM((max(count - 1, 1), now[h], rank), jnp.float32),
                pltpu.SemaphoreType.DMA((max(count - 1, 1),)),
                pltpu.SemaphoreType.DMA((max(count - 1, 1),)),
            ]
    z = shape["shard"]
    plane = shape["tensor"] * shape["dp"]
    dma = pltpu.SemaphoreType.DMA
    vmem = pl.BlockSpec(memory_space=pltpu.VMEM)
    anywhere = pl.BlockSpec(memory_space=pl.ANY)
    f32 = jnp.float32
    basis, right, following = pl.pallas_call(
        functools.partial(factors, shape),
        out_shape=[
            jax.ShapeDtypeStruct((rows, rank), f32),
            jax.ShapeDtypeStruct((cols, rank), f32),
            jax.ShapeDtypeStruct((cols, rank), f32),
        ],
        in_specs=[anywhere, anywhere, vmem],
        out_specs=[vmem, vmem, vmem],
        scratch_shapes=[
            pltpu.VMEM((rows, cols), f32),
            pltpu.VMEM((rows, cols), jnp.bfloat16),
            pltpu.VMEM((rows, rank), f32),
            pltpu.VMEM((rows, rank), f32),
            pltpu.VMEM((rank, cols), f32),
            pltpu.VMEM((2, z, rank, rank), f32),
            pltpu.VMEM((z, rank // z, cols), f32),
            pltpu.VMEM((max(z - 1, 1), rank // z, cols), f32),
            pltpu.VMEM((plane, 8, rank), f32),
            dma((2, CHUNKS)),
            dma((2, max(z - 1, 1))),
            dma((2, max(z - 1, 1))),
            dma((max(z - 1, 1),)),
            dma((max(z - 1, 1),)),
            dma((3 * halves + 1, widest)),
            dma((3 * halves + 1, widest)),
            dma((max(plane - 1, 1),)),
            dma((max(plane - 1, 1),)),
            *stages,
        ],
        compiler_params=pltpu.CompilerParams(
            collective_id=0, has_side_effects=True, vmem_limit_bytes=48 * 1024 * 1024
        ),
        name="factors",
    )(momentum, gradient, prior)

    block = rows // CHUNKS
    wide = pl.BlockSpec((block, cols), lambda i: (i, 0))
    whole = pl.BlockSpec((cols, rank), lambda i: (0, 0))
    scale = float((rows * z / rank) ** 0.5)
    momentum_next, direction = pl.pallas_call(
        functools.partial(finish, scale),
        grid=(CHUNKS,),
        out_shape=[
            jax.ShapeDtypeStruct((rows, cols), f32),
            jax.ShapeDtypeStruct((rows, cols), jnp.bfloat16),
        ],
        in_specs=[wide, wide, pl.BlockSpec((block, rank), lambda i: (i, 0)), whole, whole],
        out_specs=[wide, wide],
        name="finish",
    )(momentum, gradient, basis, right, following)
    return momentum_next[None], following[None], direction[None]


def solution(mesh):
    return jax.shard_map(
        functools.partial(shards, dict(mesh.shape)),
        mesh=mesh,
        in_specs=(
            P(None, "shard", ("tensor", "dp")),
            P(None, "shard", ("tensor", "dp")),
            P(None, ("tensor", "dp"), None),
        ),
        out_specs=(
            P(None, "shard", ("tensor", "dp")),
            P(None, ("tensor", "dp"), None),
            P(None, "shard", ("tensor", "dp")),
        ),
        check_vma=False,
    )
```

time: 304 us -> 101 us (0.33)
  waiting for transfers between devices: 165 us -> 0 us
  Pallas kernels: 0 us -> 95.1 us
  matrix products: 57.6 us -> 0 us
  other arithmetic: 49.9 us -> 0 us
  blocking collectives: 13.4 us -> 0 us
  between operations: 13.9 us -> 0.66 us
    psum x4 -> x0, waiting for transfers between devices: 165 us -> none  [the longest x2 67.3 us: summer(): return lax.psum(operand, 'shard')]
    pallas_call x0 -> x2, Pallas kernels: none -> 95.1 us  [the longest x1 82.2 us: shards(): pl.pallas_call(functools.partial(factors, shape), out_shape=[jax.ShapeDty...]
    dot_general x6 -> x0, matrix products: 54.2 us -> none  [the longest x1 17.3 us: shards(): jnp.einsum('wvp,wvc->wpc', mixed_update, column_basis, precision=lax.Prec...]
    another operation x10 -> x0, other arithmetic: 45.7 us -> none  [the longest x6 24.8 us: cholesky_pass(): factor_lower = jnp.linalg.cholesky(gram_matrix)]
    psum x1 -> x0, blocking collectives: 13.4 us -> none  [shards(): lax.psum(jnp.sum(fresh_right_factor * fresh_right_factor, axis=1), ('tens...]
    unnamed x6 -> x11, local copies, waits for them, and re-layouts: 1 us -> 4.39 us
    another operation x2 -> x0, matrix products: 3.34 us -> none  [cholesky_pass(): lax.linalg.triangular_solve(factor_lower, row_segment_block, left_side=Fa...]
  transfers between devices with their start and end apart: 4 -> 0, of which waited for: 4 -> 0; matrix products, arithmetic and copies ran while one was open for 0% -> 0% of each run, Pallas kernels for 0% -> 0%
where the time goes in v1:
time: 101 us; the launch traced here: 100 us
  Pallas kernels  95.1 us (94%)
  local copies, waits for them, and re-layouts  4.39 us (4%)
    pallas_call x1, Pallas kernels, shards(): pl.pallas_call(functools.partial(factors, shape), out_shape=[jax.ShapeDty...  82.2 us
    pallas_call x1, Pallas kernels, shards(): pl.pallas_call(functools.partial(finish, scale), grid=(CHUNKS,), out_shap...  12.9 us
    unnamed x11, local copies, waits for them, and re-layouts  4.39 us

profile of v1, /device:TPU:0, one launch (start us, length us, event | category | flops | bytes accessed | tf_op | source)
XLA Modules:
  0.0 100.2 jit_solution(6008259551123090456)
XLA Ops:
  0.6 0.0 copy-start.3
  0.6 1.0 %copy-done.3 = f32[1,1024,128]{2,1,0:T(8,128)S(1)} copy-done((f32[1,1024,128]{2,1,0:T(8,128)S(1)}, f32[1,1024,128]{2,1,0:T(8,128)}, u32[]{:S(2)}) %copy-start.3) | copy-done | bytes 524312
  1.7 82.2 %factors.1 = (f32[2048,128]{1,0:T(8,128)S(1)}, f32[1024,128]{1,0:T(8,128)S(1)}, f32[1024,128]{1,0:T(8,128)S(1)}) custom-call(f32[2048,1024]{1,0:T(8,128)} %bitcast.8, bf16[2048,1024]{1,0:T(8,128)(2,1)} %bitcast.10, f32[1024,128]{1,0:T(8,128)S(1)} %bitcast.7), custom_call_target="tpu_custom_call" | custom-call | tf_op jit(solution)/shard_map/factors/pallas_call | solution.py:313
  83.9 0.0 copy-start
  83.9 0.8 copy-done
  84.7 0.0 copy-start.2
  84.7 1.0 copy-done.2
  85.7 0.0 copy-start.4
  85.7 0.8 copy-done.4
  86.5 0.0 copy-start.1
  86.5 12.9 %finish.1 = (f32[2048,1024]{1,0:T(8,128)}, bf16[2048,1024]{1,0:T(8,128)(2,1)}) custom-call(f32[2048,1024]{1,0:T(8,128)} %bitcast.9, bf16[2048,1024]{1,0:T(8,128)(2,1)} %bitcast.11, f32[2048,128]{1,0:T(8,128)} %copy-done.2, f32[1024,128]{1,0:T(8,128)} %copy-done.4, f32[1024,128]{1,0:T(8,128)} %copy-done), custom_call_target="tpu_custom_call" | custom-call | tf_op jit(solution)/shard_map/finish/pallas_call | solution.py:353
  99.4 0.0 copy-done.1
  99.4 0.8 copy.7
Async XLA Ops:
  0.6 1.0 %copy-start.3 = (f32[1,1024,128]{2,1,0:T(8,128)S(1)}, f32[1,1024,128]{2,1,0:T(8,128)}, u32[]{:S(2)}) copy-start(f32[1,1024,128]{2,1,0:T(8,128)} %param.5) | copy-start | bytes 1572868
  83.9 0.8 copy-start
  84.7 1.0 copy-start.2
  85.7 0.8 copy-start.4
  86.5 12.9 %copy-start.1 = (f32[1024,128]{1,0:T(8,128)S(1)}, f32[1024,128]{1,0:T(8,128)}, u32[]{:S(2)}) copy-start(f32[1024,128]{1,0:T(8,128)} %copy-done) | copy-start | bytes 1572868

commit v2 on v1

--- a/solution.py
+++ b/solution.py
@@ -24,6 +24,14 @@
     high = value.astype(jnp.bfloat16)
     low = (value - high.astype(jnp.float32)).astype(jnp.bfloat16)
     return high, low
+
+
+def product(lhs, rhs):
+    high, low = split(lhs)
+    pair = jnp.concatenate(split(rhs), axis=1)
+    both = dot(high, pair, ((1,), (0,)), None) + dot(low, pair, ((1,), (0,)), None)
+    width = rhs.shape[1]
+    return both[:, :width] + both[:, width:]
 
 
 def inverse_factor(gram):
@@ -99,7 +107,8 @@
 
 
 def factors(shape, momentum_ref, gradient_ref, prior_ref, basis_ref, right_ref, following_ref, *scratch):
-    (mixed, raw, left, whole, local, grams, shares, share_in, squares, load_sem, gram_send, gram_recv, share_send,
+    (mixed, raw, left, whole, local, pieces, piece_in, piece_z, piece_all, shares, share_in, squares, load_sem,
+     gram_send, gram_recv, share_send,
      share_recv, full_send, full_recv, square_send, square_recv, *stages) = scratch
     rows, cols = mixed.shape
     rank = prior_ref.shape[1]
@@ -126,6 +135,54 @@
             peers += 1
     pl.semaphore_wait(barrier, peers)
 
+    plane, z = where["plane"], where["z"]
+    piece = rank // plane.count
+
+    def summed(slots, count):
+        total = slots[0]
+        for i in range(1, count):
+            total = total + slots[i]
+        return total
+
+    def sends(group, turn, stage, source, target):
+        copies = []
+        for k in range(1, group.count):
+            other, device = group.peer(k)
+            copy = pltpu.make_async_remote_copy(
+                src_ref=source(other),
+                dst_ref=target,
+                send_sem=gram_send.at[turn, stage, k - 1],
+                recv_sem=gram_recv.at[turn, stage, k - 1],
+                device_id=device,
+                device_id_type=MESH,
+            )
+            copy.start()
+            copies.append(copy)
+        return copies
+
+    def gram_steps(turn, values):
+        gram = sum(dot(value, value, ((0,), (0,))) for value in values)
+        for i in range(plane.count):
+            pieces[turn, i] = gram[i * piece : (i + 1) * piece]
+        piece_in[turn, plane.me] = pieces[turn, plane.me]
+        copies = sends(plane, turn, 0, lambda i: pieces.at[turn, i], piece_in.at[turn, plane.me])
+        yield
+        for copy in copies:
+            copy.wait()
+        piece_z[turn, z.me] = summed(piece_in.at[turn], plane.count)
+        own = piece_z.at[turn, z.me]
+        copies = sends(z, turn, 1, lambda i: own, own)
+        yield
+        for copy in copies:
+            copy.wait()
+        piece_all[turn, plane.me] = summed(piece_z.at[turn], z.count)
+        own = piece_all.at[turn, plane.me]
+        copies = sends(plane, turn, 2, lambda i: own, own)
+        yield
+        for copy in copies:
+            copy.wait()
+        yield jnp.concatenate([piece_all[turn, i] for i in range(plane.count)], axis=0)
+
     prior = prior_ref[...]
 
     def first(i, carry):
@@ -134,7 +191,7 @@
         at = pl.ds(pl.multiple_of(i * part, 8), part)
         value = mixed[at, :] + raw[at, :].astype(jnp.float32)
         mixed[at, :] = value
-        left[at, :] = dot(value, prior, ((1,), (0,)))
+        left[at, :] = product(value, prior)
         return carry
 
     lax.fori_loop(0, CHUNKS, first, 0)
@@ -197,6 +254,19 @@
                 )
                 copy.start()
                 copies.append(copy)
+        if level == 2:
+            steps = gram_steps(0, [left[pl.ds(starts[h], sizes_now[h]), :] for h in range(halves)])
+            next(steps)
+        elif level == 1:
+            next(steps)
+        else:
+            next(steps)
+            inverse = inverse_factor(next(steps))
+            owned = [
+                dot(left[pl.ds(starts[h], sizes_now[h]), :], inverse, ((1,), (1,))) for h in range(halves)
+            ]
+            steps = gram_steps(1, owned)
+            next(steps)
         for copy in copies:
             copy.wait()
 
@@ -215,24 +285,19 @@
             copies.append(copy)
         return copies
 
-    def summed(slots, count):
-        total = slots[0]
-        for i in range(1, count):
-            total = total + slots[i]
-        return total
-
-    z = where["z"]
-    value = whole[...]
-    grams[0, z.me] = dot(value, value, ((0,), (0,)))
-    for copy in exchange(grams.at[0], z, gram_send.at[0], gram_recv.at[0]):
-        copy.wait()
-    inverse = inverse_factor(summed(grams.at[0], z.count))
     value = dot(whole[...], inverse, ((1,), (1,)))
     basis_ref[...] = value
-    grams[1, z.me] = dot(value, value, ((0,), (0,)))
-    gram_copies = exchange(grams.at[1], z, gram_send.at[1], gram_recv.at[1])
-
-    local[...] = dot(value, mixed[...], ((0,), (0,)))
+    next(steps)
+    high, low = split(value)
+    half = cols // 2
+    for c in range(2):
+        wide_high, wide_low = split(mixed[:, c * half : (c + 1) * half])
+        both = dot(jnp.concatenate([high, low], axis=1), wide_high, ((0,), (0,)), None)
+        local[:, c * half : (c + 1) * half] = (
+            both[:rank] + both[rank:] + dot(high, wide_low, ((0,), (0,)), None)
+        )
+        if c == 0:
+            next(steps)
     share = rank // z.count
     share_copies = []
     for k in range(1, z.count):
@@ -247,9 +312,7 @@
         )
         copy.start()
         share_copies.append(copy)
-    for copy in gram_copies:
-        copy.wait()
-    inverse = inverse_factor(summed(grams.at[1], z.count))
+    inverse = inverse_factor(next(steps))
     for copy in share_copies:
         copy.wait()
     total = local[pl.ds(pl.multiple_of(z.me * share, 8), share), :]
@@ -263,7 +326,6 @@
     stacked = jnp.concatenate([shares[i] for i in range(z.count)], axis=0)
     right = dot(stacked, inverse, ((0,), (1,)))
     right_ref[...] = right
-    plane = where["plane"]
     squares[plane.me] = jnp.broadcast_to(jnp.sum(right * right, axis=0, keepdims=True), (8, rank))
     for copy in exchange(squares, plane, square_send, square_recv):
         copy.wait()
@@ -325,13 +387,16 @@
             pltpu.VMEM((rows, rank), f32),
             pltpu.VMEM((rows, rank), f32),
             pltpu.VMEM((rank, cols), f32),
-            pltpu.VMEM((2, z, rank, rank), f32),
+            pltpu.VMEM((2, plane, rank // plane, rank), f32),
+            pltpu.VMEM((2, plane, rank // plane, rank), f32),
+            pltpu.VMEM((2, z, rank // plane, rank), f32),
+            pltpu.VMEM((2, plane, rank // plane, rank), f32),
             pltpu.VMEM((z, rank // z, cols), f32),
             pltpu.VMEM((max(z - 1, 1), rank // z, cols), f32),
             pltpu.VMEM((plane, 8, rank), f32),
             dma((2, CHUNKS)),
-            dma((2, max(z - 1, 1))),
-            dma((2, max(z - 1, 1))),
+            dma((2, 3, max(plane, z))),
+            dma((2, 3, max(plane, z))),
             dma((max(z - 1, 1),)),
             dma((max(z - 1, 1),)),
             dma((3 * halves + 1, widest)),

time: 101 us -> 91 us (0.901)
  Pallas kernels: 95.1 us -> 85.7 us
    pallas_call x1, Pallas kernels: 82.2 us -> 72.8 us  [shards(): pl.pallas_call(functools.partial(factors, shape), out_shape=[jax.ShapeDty...]
where the time goes in v2:
time: 91 us; the launch traced here: 90.7 us
  Pallas kernels  85.7 us (94%)
  local copies, waits for them, and re-layouts  4.39 us (5%)
    pallas_call x1, Pallas kernels, shards(): pl.pallas_call(functools.partial(factors, shape), out_shape=[jax.ShapeDty...  72.8 us
    pallas_call x1, Pallas kernels, shards(): pl.pallas_call(functools.partial(finish, scale), grid=(CHUNKS,), out_shap...  12.9 us
    unnamed x11, local copies, waits for them, and re-layouts  4.39 us

profile of v2, /device:TPU:0, one launch (start us, length us, event | category | flops | bytes accessed | tf_op | source)
XLA Modules:
  0.0 90.7 jit_solution(1014209413866379586)
XLA Ops:
  0.6 0.0 copy-start.3
  0.6 1.0 %copy-done.3 = f32[1,1024,128]{2,1,0:T(8,128)S(1)} copy-done((f32[1,1024,128]{2,1,0:T(8,128)S(1)}, f32[1,1024,128]{2,1,0:T(8,128)}, u32[]{:S(2)}) %copy-start.3) | copy-done | bytes 524312
  1.7 72.8 %factors.1 = (f32[2048,128]{1,0:T(8,128)S(1)}, f32[1024,128]{1,0:T(8,128)S(1)}, f32[1024,128]{1,0:T(8,128)S(1)}) custom-call(f32[2048,1024]{1,0:T(8,128)} %bitcast.8, bf16[2048,1024]{1,0:T(8,128)(2,1)} %bitcast.10, f32[1024,128]{1,0:T(8,128)S(1)} %bitcast.7), custom_call_target="tpu_custom_call" | custom-call | tf_op jit(solution)/shard_map/factors/pallas_call | solution.py:375
  74.5 0.0 copy-start
  74.5 0.8 copy-done
  75.3 0.0 copy-start.2
  75.3 1.0 %copy-done.2 = f32[2048,128]{1,0:T(8,128)} copy-done((f32[2048,128]{1,0:T(8,128)}, f32[2048,128]{1,0:T(8,128)S(1)}, u32[]{:S(2)}) %copy-start.2) | copy-done | bytes 1048600
  76.2 0.0 copy-start.4
  76.2 0.8 copy-done.4
  77.0 0.0 copy-start.1
  77.0 12.9 %finish.1 = (f32[2048,1024]{1,0:T(8,128)}, bf16[2048,1024]{1,0:T(8,128)(2,1)}) custom-call(f32[2048,1024]{1,0:T(8,128)} %bitcast.9, bf16[2048,1024]{1,0:T(8,128)(2,1)} %bitcast.11, f32[2048,128]{1,0:T(8,128)} %copy-done.2, f32[1024,128]{1,0:T(8,128)} %copy-done.4, f32[1024,128]{1,0:T(8,128)} %copy-done), custom_call_target="tpu_custom_call" | custom-call | tf_op jit(solution)/shard_map/finish/pallas_call | solution.py:418
  89.9 0.0 copy-done.1
  89.9 0.8 copy.7
Async XLA Ops:
  0.6 1.0 %copy-start.3 = (f32[1,1024,128]{2,1,0:T(8,128)S(1)}, f32[1,1024,128]{2,1,0:T(8,128)}, u32[]{:S(2)}) copy-start(f32[1,1024,128]{2,1,0:T(8,128)} %param.5) | copy-start | bytes 1572868
  74.5 0.8 copy-start
  75.3 1.0 %copy-start.2 = (f32[2048,128]{1,0:T(8,128)}, f32[2048,128]{1,0:T(8,128)S(1)}, u32[]{:S(2)}) copy-start(f32[2048,128]{1,0:T(8,128)S(1)} %get-tuple-element.8.basis_ref) | copy-start | bytes 3145732
  76.2 0.8 copy-start.4
  77.0 12.9 %copy-start.1 = (f32[1024,128]{1,0:T(8,128)S(1)}, f32[1024,128]{1,0:T(8,128)}, u32[]{:S(2)}) copy-start(f32[1024,128]{1,0:T(8,128)} %copy-done) | copy-start | bytes 1572868

commit v3 on v2

--- a/solution.py
+++ b/solution.py
@@ -12,6 +12,7 @@
 decay_rate = 0.95
 epsilon = 1e-06
 CHUNKS = 8
+STEPS = 4
 
 
 def dot(a, b, dims, precision=HIGHEST):
@@ -109,7 +110,8 @@
 def factors(shape, momentum_ref, gradient_ref, prior_ref, basis_ref, right_ref, following_ref, *scratch):
     (mixed, raw, left, whole, local, pieces, piece_in, piece_z, piece_all, shares, share_in, squares, load_sem,
      gram_send, gram_recv, share_send,
-     share_recv, full_send, full_recv, square_send, square_recv, *stages) = scratch
+     share_recv, full_send, full_recv, square_send, square_recv, prior_vmem,
+     prior_sem, *stages) = scratch
     rows, cols = mixed.shape
     rank = prior_ref.shape[1]
     where = groups(shape)
@@ -123,6 +125,8 @@
             pltpu.make_async_copy(gradient_ref.at[at], raw.at[at], load_sem.at[1, i]),
         )
 
+    prior_copy = pltpu.make_async_copy(prior_ref, prior_vmem, prior_sem)
+    prior_copy.start()
     for i in range(CHUNKS):
         for copy in load(i):
             copy.start()
@@ -183,7 +187,8 @@
             copy.wait()
         yield jnp.concatenate([piece_all[turn, i] for i in range(plane.count)], axis=0)
 
-    prior = prior_ref[...]
+    prior_copy.wait()
+    prior = prior_vmem[...]
 
     def first(i, carry):
         for copy in load(i):
@@ -343,9 +348,9 @@
         + gradient_ref[...].astype(jnp.float32)
         - (1.0 - decay_rate) * dot(high, right, dims, None)
     )
-    product = dot(high, follow_high, dims, None) + (
-        dot(high, follow_low, dims, None) + dot(low, follow_high, dims, None)
-    )
+    product = dot(
+        jnp.concatenate([high, low], axis=1), jnp.concatenate([follow_high, follow_high], axis=1), dims, None
+    ) + dot(high, follow_low, dims, None)
     direction_ref[...] = (scale * product).astype(jnp.bfloat16)
 
 
@@ -379,7 +384,7 @@
             jax.ShapeDtypeStruct((cols, rank), f32),
             jax.ShapeDtypeStruct((cols, rank), f32),
         ],
-        in_specs=[anywhere, anywhere, vmem],
+        in_specs=[anywhere, anywhere, anywhere],
         out_specs=[vmem, vmem, vmem],
         scratch_shapes=[
             pltpu.VMEM((rows, cols), f32),
@@ -403,6 +408,8 @@
             dma((3 * halves + 1, widest)),
             dma((max(plane - 1, 1),)),
             dma((max(plane - 1, 1),)),
+            pltpu.VMEM((cols, rank), f32),
+            dma,
             *stages,
         ],
         compiler_params=pltpu.CompilerParams(
@@ -411,13 +418,13 @@
         name="factors",
     )(momentum, gradient, prior)
 
-    block = rows // CHUNKS
+    block = rows // STEPS
     wide = pl.BlockSpec((block, cols), lambda i: (i, 0))
     whole = pl.BlockSpec((cols, rank), lambda i: (0, 0))
     scale = float((rows * z / rank) ** 0.5)
     momentum_next, direction = pl.pallas_call(
         functools.partial(finish, scale),
-        grid=(CHUNKS,),
+        grid=(STEPS,),
         out_shape=[
             jax.ShapeDtypeStruct((rows, cols), f32),
             jax.ShapeDtypeStruct((rows, cols), jnp.bfloat16),

time: 91 us -> 88.5 us (0.973)
  Pallas kernels: 85.7 us -> 83.3 us
    pallas_call x1, Pallas kernels: 12.9 us -> 10.4 us  [shards(): pl.pallas_call(functools.partial(finish, scale), grid=(STEPS,), out_shape...]
where the time goes in v3:
time: 88.5 us; the launch traced here: 88.3 us
  Pallas kernels  83.3 us (94%)
  local copies, waits for them, and re-layouts  4.39 us (5%)
    pallas_call x1, Pallas kernels, shards(): pl.pallas_call(functools.partial(factors, shape), out_shape=[jax.ShapeDty...  72.8 us
    pallas_call x1, Pallas kernels, shards(): pl.pallas_call(functools.partial(finish, scale), grid=(STEPS,), out_shape...  10.4 us
    unnamed x11, local copies, waits for them, and re-layouts  4.39 us

profile of v3, /device:TPU:0, one launch (start us, length us, event | category | flops | bytes accessed | tf_op | source)
XLA Modules:
  0.0 88.3 jit_solution(1300629623266096704)
XLA Ops:
  0.6 0.0 copy-start.3
  0.6 1.0 %copy-done.3 = f32[1,1024,128]{2,1,0:T(8,128)S(1)} copy-done((f32[1,1024,128]{2,1,0:T(8,128)S(1)}, f32[1,1024,128]{2,1,0:T(8,128)}, u32[]{:S(2)}) %copy-start.3) | copy-done | bytes 524312
  1.7 72.8 %factors.1 = (f32[2048,128]{1,0:T(8,128)S(1)}, f32[1024,128]{1,0:T(8,128)S(1)}, f32[1024,128]{1,0:T(8,128)S(1)}) custom-call(f32[2048,1024]{1,0:T(8,128)} %bitcast.8, bf16[2048,1024]{1,0:T(8,128)(2,1)} %bitcast.10, f32[1024,128]{1,0:T(8,128)S(1)} %bitcast.7), custom_call_target="tpu_custom_call" | custom-call | tf_op jit(solution)/shard_map/factors/pallas_call | solution.py:380
  74.5 0.0 copy-start
  74.5 0.8 copy-done
  75.3 0.0 copy-start.2
  75.3 1.0 %copy-done.2 = f32[2048,128]{1,0:T(8,128)} copy-done((f32[2048,128]{1,0:T(8,128)}, f32[2048,128]{1,0:T(8,128)S(1)}, u32[]{:S(2)}) %copy-start.2) | copy-done | bytes 1048600
  76.3 0.0 copy-start.4
  76.3 0.8 copy-done.4
  77.1 0.0 copy-start.1
  77.1 10.4 %finish.1 = (f32[2048,1024]{1,0:T(8,128)}, bf16[2048,1024]{1,0:T(8,128)(2,1)}) custom-call(f32[2048,1024]{1,0:T(8,128)} %bitcast.9, bf16[2048,1024]{1,0:T(8,128)(2,1)} %bitcast.11, f32[2048,128]{1,0:T(8,128)} %copy-done.2, f32[1024,128]{1,0:T(8,128)} %copy-done.4, f32[1024,128]{1,0:T(8,128)} %copy-done), custom_call_target="tpu_custom_call" | custom-call | tf_op jit(solution)/shard_map/finish/pallas_call | solution.py:425
  87.5 0.0 copy-done.1
  87.5 0.8 copy.7
Async XLA Ops:
  0.6 1.0 %copy-start.3 = (f32[1,1024,128]{2,1,0:T(8,128)S(1)}, f32[1,1024,128]{2,1,0:T(8,128)}, u32[]{:S(2)}) copy-start(f32[1,1024,128]{2,1,0:T(8,128)} %param.5) | copy-start | bytes 1572868
  74.5 0.8 copy-start
  75.3 1.0 %copy-start.2 = (f32[2048,128]{1,0:T(8,128)}, f32[2048,128]{1,0:T(8,128)S(1)}, u32[]{:S(2)}) copy-start(f32[2048,128]{1,0:T(8,128)S(1)} %get-tuple-element.8.basis_ref) | copy-start | bytes 3145732
  76.3 0.8 copy-start.4
  77.1 10.4 %copy-start.1 = (f32[1024,128]{1,0:T(8,128)S(1)}, f32[1024,128]{1,0:T(8,128)}, u32[]{:S(2)}) copy-start(f32[1024,128]{1,0:T(8,128)} %copy-done) | copy-start | bytes 1572868
